TPU v7x, 32 devices: a whole 2x2x4 slice. The times are simulated.
32 devices in a mesh: gx: 4 (over z), gy: 8 (over y, x, core).
Axes of the slice: x: 2, y: 2, z: 4, core: 2. Of those that a mesh axis runs over, the one named last changes fastest.
Arguments:
- die_basis: float32 [64, 256, 512], P('gx', 'gy'), may hold values from -0.078125 to 0.078125
- die_coeff: float32 [5, 64, 256], P(None, 'gx', 'gy'), may hold values from 0.2 to 5
- pkg_basis: float32 [1024, 64, 512], P(('gx', 'gy')), may hold values from -0.09375 to 0.09375
- send_blocks: int32 [32, 4, 4], P(('gx', 'gy')), may hold values from 0 to 31
- columns: int32 [5, 1024, 4], P(None, ('gx', 'gy')), may hold values from 0 to 47
- counts: int32 [5, 1024], P(None, ('gx', 'gy')), may hold values from 1 to 4
- pkg_blocks: float32 [5, 1024, 64, 256], P(None, ('gx', 'gy')), may hold values from -48 to 48
Outputs:
- reduced: float32 [5, 512, 512], replicated
Inputs may be any that keep to these rules, and one draw needn't show every extreme that they name: `columns`: indices below 32 name the partition's own blocks, the others its ghost blocks in the order of the statement.
All inputs are finite; a program needn't handle non-finite values.
Results may differ from a plain program's by a relative error of at most 0.0001.
Values sent between devices are 32-bit elements; how exact they have to be, the bound alone decides.
No kernel may reach another device: no remote copies, remote signals or barrier semaphores. Data moves between devices by JAX's collectives and lax.ppermute only.
A program may use at most 256 MiB of HBM per device.

v0:
```python
import jax
import jax.numpy as jnp
from jax import lax
from jax.sharding import PartitionSpec as P

highest = lax.Precision.HIGHEST


def from_behind(value, axis, steps):
    count = lax.axis_size(axis)
    leading, last = (max(0, -steps), min(count, count - steps))
    return lax.ppermute(value, axis, [(source, source + steps) for source in range(leading, last)])


def passed_along(value, axis, steps):
    count = lax.axis_size(axis)
    pairs = [(source, (source + steps) % count) for source in range(count)]
    return lax.ppermute(value, axis, pairs)


def weighted_gram(weights, field):
    width = field.shape[-1]
    flat = field.reshape(-1, width)
    scaled = weights.reshape(-1, 1) * flat
    return lax.dot_general(
        flat,
        scaled,
        (((0,), (0,)), ((), ())),
        precision=highest,
        preferred_element_type=jnp.float32,
    )


def die_terms(basis, coeff, next_x_row, next_y_col):
    next_x = jnp.concatenate([basis[1:], next_x_row], axis=0)
    next_y = jnp.concatenate([basis[:, 1:], next_y_col], axis=1)
    diff_x = basis - next_x
    diff_y = basis - next_y
    return jnp.stack(
        [
            weighted_gram(coeff[0], basis),
            weighted_gram(coeff[1], diff_x),
            weighted_gram(coeff[2], diff_y),
            weighted_gram(coeff[3], basis),
            weighted_gram(coeff[4], diff_x) + weighted_gram(coeff[4], diff_y),
        ]
    )


def package_terms(owned, table, columns, counts, blocks):
    row_count = owned.shape[0]
    block = owned.shape[1]
    width = owned.shape[2]
    entries = columns.shape[-1]
    results = []
    for term_idx in range(columns.shape[0]):
        picked = table[columns[term_idx]]
        live = (jnp.arange(entries, dtype=jnp.int32)[None, :] < counts[term_idx][:, None]).astype(
            jnp.float32
        )
        matrices = (
            blocks[term_idx].reshape(row_count, block, entries, block) * live[:, None, :, None]
        )
        image = jnp.einsum("rinj,rnjk->rik", matrices, picked, precision=highest)
        results.append(
            lax.dot_general(
                owned.reshape(-1, width),
                image.reshape(-1, width),
                (((0,), (0,)), ((), ())),
                precision=highest,
                preferred_element_type=jnp.float32,
            )
        )
    return jnp.stack(results)


def body(die_basis, die_coeff, pkg_basis, send_blocks, columns, counts, pkg_blocks):
    next_x_row = from_behind(die_basis[:1], "gx", -1)
    next_y_col = from_behind(die_basis[:, :1], "gy", -1)
    lists = send_blocks[0]
    from_lower_x = passed_along(pkg_basis[lists[0]], "gx", 1)
    from_upper_x = passed_along(pkg_basis[lists[1]], "gx", -1)
    from_lower_y = passed_along(pkg_basis[lists[2]], "gy", 1)
    from_upper_y = passed_along(pkg_basis[lists[3]], "gy", -1)
    table = jnp.concatenate(
        [pkg_basis, from_lower_x, from_upper_x, from_lower_y, from_upper_y], axis=0
    )
    partial_terms = die_terms(die_basis, die_coeff, next_x_row, next_y_col)
    partial_terms = partial_terms + package_terms(pkg_basis, table, columns, counts, pkg_blocks)
    return lax.psum(partial_terms, ("gx", "gy"))


def solution(mesh):
    placed = (
        P("gx", "gy", None),
        P(None, "gx", "gy"),
        P(("gx", "gy"), None, None),
        P(("gx", "gy"), None, None),
        P(None, ("gx", "gy"), None),
        P(None, ("gx", "gy")),
        P(None, ("gx", "gy"), None, None),
    )
    return jax.shard_map(body, mesh=mesh, in_specs=placed, out_specs=P(), check_vma=False)
```

profile of v0, /device:TPU:0, one launch (start us, length us, event | category | flops | bytes accessed | tf_op | source)
XLA Modules:
  0.0 460.3 jit_solution(5091545625883094443)
XLA Ops:
  7.4 3.6 gather_fusion
  11.0 3.1 collective-permute-start.2
  14.0 3.6 gather_fusion.1
  17.6 2.0 collective-permute-start.3
  19.6 3.6 gather_fusion.2
  23.2 3.6 gather_fusion.3
  26.8 2.6 collective-permute-start.5
  30.8 4.9 %constant_dynamic-update-slice_fusion.4 = f32[48,64,512]{2,1,0:T(8,128)} fusion(f32[32,64,512]{2,1,0:T(8,128)} %param.9), kind=kLoop, calls=%fused_computation.81 | loop fusion | bytes 8388608
  36.1 7.9 %fusion.120 = (f32[1,32,64,256]{3,2,1,0:T(8,128)S(1)}, f32[1,32,64,256]{3,2,1,0:T(8,128)}, f32[1,32,64,256]{3,2,1,0:T(8,128)}, f32[1,32,64,256]{3,2,1,0:T(8,128)}, f32[1,32,64,256]{3,2,1,0:T(8,128)}) fusion(f32[5,32,64,256]{3,2,1,0:T(8,128)} %param.13), kind=kLoop, calls=%fused_computation.128 | loop fusion | bytes 20971520 | tf_op jit(solution)/shard_map/slice | solution.py:62
  44.0 5.1 %reshape_squeeze.22 = f32[32,64,4,64]{3,2,1,0:T(4,128)} reshape(f32[1,32,64,256]{3,2,1,0:T(8,128)} %get-tuple-element.7) | data formatting | bytes 4194304 | tf_op jit(solution)/shard_map/reshape;squeeze | solution.py:62
  49.3 5.1 %reshape_squeeze.10 = f32[32,64,4,64]{3,2,1,0:T(4,128)} reshape(f32[1,32,64,256]{3,2,1,0:T(8,128)} %get-tuple-element.8) | data formatting | bytes 4194304 | tf_op jit(solution)/shard_map/reshape;squeeze | solution.py:62
  54.3 5.1 %reshape_squeeze.23 = f32[32,64,4,64]{3,2,1,0:T(4,128)} reshape(f32[1,32,64,256]{3,2,1,0:T(8,128)} %get-tuple-element.6) | data formatting | bytes 4194304 | tf_op jit(solution)/shard_map/reshape;squeeze | solution.py:62
  59.8 5.1 %reshape_squeeze.24 = f32[32,64,4,64]{3,2,1,0:T(4,128)} reshape(f32[1,32,64,256]{3,2,1,0:T(8,128)} %get-tuple-element.9) | data formatting | bytes 4194304 | tf_op jit(solution)/shard_map/reshape;squeeze | solution.py:62
  64.9 3.5 reshape_squeeze.25
  68.5 2.0 fusion.35
  70.6 2.9 broadcast_multiply_fusion.3
  73.5 2.9 broadcast_multiply_fusion.4
  76.6 2.9 broadcast_multiply_fusion.2
  79.5 2.9 broadcast_multiply_fusion.1
  82.5 3.0 broadcast_multiply_fusion
  87.2 2.2 fusion.59
  89.4 3.0 collective-permute-done
  92.4 2.1 fusion.41
  94.5 2.2 fusion.47
  96.8 2.0 fusion.53
  98.8 2.2 fusion.98
  101.0 2.3 copy-done.10
  105.2 1.9 constant_dynamic-update-slice_fusion.2
  107.1 1.9 constant_dynamic-update-slice_fusion.1
  109.0 1.9 constant_dynamic-update-slice_fusion
  110.8 12.9 %gather_fusion.5 = f32[128,64,512]{2,1,0:T(8,128)} fusion(f32[48,64,512]{2,1,0:T(8,128)} %constant_dynamic-update-slice_fusion, s32[1024]{0:T(1024)S(1)} %get-tuple-element.32), kind=kCustom, calls=%fused_computation.5 | custom fusion | bytes 33554944 | tf_op jit(solution)/shard_map/gather | solution.py:57
  123.7 12.7 %gather_fusion.4 = f32[128,64,512]{2,1,0:T(8,128)} fusion(f32[48,64,512]{2,1,0:T(8,128)} %constant_dynamic-update-slice_fusion, s32[1024]{0:T(1024)S(1)} %pad_clamp_fusion.4), kind=kCustom, calls=%fused_computation.4 | custom fusion | bytes 33554944 | tf_op jit(solution)/shard_map/gather | solution.py:57
  136.4 13.9 %fusion.18 = f32[32,64,512,1]{2,1,3,0:T(8,128)S(1)} fusion(f32[32,4,64,512]{3,2,1,0:T(8,128)} %bitcast.211, f32[32,64,4,64]{3,2,1,0:T(4,128)} %broadcast_multiply_fusion.4), kind=kOutput, calls=%fused_computation.27 | convolution fusion | flops 3221225472 | bytes 23068672 | tf_op jit(solution)/shard_map/rinj,rnjk->rik/dot_general | solution.py:64
  150.4 8.0 %fusion.65 = f32[5,512,512]{1,2,0:T(8,128)} fusion(f32[32,64,512]{2,1,0:T(8,128)S(1)} %copy-done.9, f32[32,64,512,1]{2,1,3,0:T(8,128)S(1)} %fusion.18), kind=kOutput, calls=%fused_computation.57 | convolution fusion | flops 6442450944 | bytes 9437184 | tf_op jit(solution)/shard_map/dot_general | solution.py:66
  158.3 12.7 %gather_fusion.6 = f32[128,64,512]{2,1,0:T(8,128)} fusion(f32[48,64,512]{2,1,0:T(8,128)} %constant_dynamic-update-slice_fusion, s32[1024]{0:T(1024)S(1)} %get-tuple-element.31), kind=kCustom, calls=%fused_computation.6 | custom fusion | bytes 33554944 | tf_op jit(solution)/shard_map/gather | solution.py:57
  171.0 12.7 %gather_fusion.7 = f32[128,64,512]{2,1,0:T(8,128)} fusion(f32[48,64,512]{2,1,0:T(8,128)} %constant_dynamic-update-slice_fusion, s32[1024]{0:T(1024)S(1)} %get-tuple-element.30), kind=kCustom, calls=%fused_computation.7 | custom fusion | bytes 33554944 | tf_op jit(solution)/shard_map/gather | solution.py:57
  183.7 12.9 %gather_fusion.8 = f32[128,64,512]{2,1,0:T(8,128)} fusion(f32[48,64,512]{2,1,0:T(8,128)} %constant_dynamic-update-slice_fusion, s32[1024]{0:T(1024)S(1)} %get-tuple-element.29), kind=kCustom, calls=%fused_computation.8 | custom fusion | bytes 33554944 | tf_op jit(solution)/shard_map/gather | solution.py:57
  196.5 16.1 %fusion.16 = f32[32,64,512,1]{2,1,3,0:T(8,128)} fusion(f32[32,4,64,512]{3,2,1,0:T(8,128)} %bitcast.206, f32[32,64,4,64]{3,2,1,0:T(4,128)} %broadcast_multiply_fusion.3), kind=kOutput, calls=%fused_computation.25 | convolution fusion | flops 3221225472 | bytes 23068672 | tf_op jit(solution)/shard_map/rinj,rnjk->rik/dot_general | solution.py:64
  212.6 10.4 %fusion.71 = f32[5,512,512]{1,2,0:T(8,128)} fusion(f32[5,512,512]{1,2,0:T(8,128)} %fusion.65, f32[32,64,512]{2,1,0:T(8,128)} %param.9, f32[32,64,512,1]{2,1,3,0:T(8,128)} %fusion.16), kind=kOutput, calls=%fused_computation.59 | convolution fusion | flops 6442450944 | bytes 9437184 | tf_op jit(solution)/shard_map/dot_general | solution.py:66
  223.0 12.0 %fusion.14 = f32[32,64,512,1]{2,1,3,0:T(8,128)} fusion(f32[32,4,64,512]{3,2,1,0:T(8,128)S(1)} %bitcast.210, f32[32,64,4,64]{3,2,1,0:T(4,128)S(1)} %copy-done.6), kind=kOutput, calls=%fused_computation.23 | convolution fusion | flops 3221225472 | bytes 23068672 | tf_op jit(solution)/shard_map/rinj,rnjk->rik/dot_general | solution.py:64
  235.1 10.4 %fusion.77 = f32[5,512,512]{1,2,0:T(8,128)} fusion(f32[5,512,512]{1,2,0:T(8,128)} %fusion.71, f32[32,64,512]{2,1,0:T(8,128)} %param.9, f32[32,64,512,1]{2,1,3,0:T(8,128)} %fusion.14), kind=kOutput, calls=%fused_computation.61 | convolution fusion | flops 6442450944 | bytes 9437184 | tf_op jit(solution)/shard_map/dot_general | solution.py:66
  245.5 14.7 %fusion.12 = f32[32,64,512,1]{2,1,3,0:T(8,128)} fusion(f32[32,4,64,512]{3,2,1,0:T(8,128)} %bitcast.207, f32[32,64,4,64]{3,2,1,0:T(4,128)S(1)} %copy-done.8), kind=kOutput, calls=%fused_computation.21 | convolution fusion | flops 3221225472 | bytes 23068672 | tf_op jit(solution)/shard_map/rinj,rnjk->rik/dot_general | solution.py:64
  260.2 10.6 %fusion.83 = f32[5,512,512]{1,2,0:T(8,128)} fusion(f32[5,512,512]{1,2,0:T(8,128)} %fusion.77, f32[32,64,512]{2,1,0:T(8,128)} %param.9, f32[32,64,512,1]{2,1,3,0:T(8,128)} %fusion.12), kind=kOutput, calls=%fused_computation.63 | convolution fusion | flops 6442450944 | bytes 9437184 | tf_op jit(solution)/shard_map/dot_general | solution.py:66
  270.8 11.8 %fusion.10 = f32[32,64,512,1]{2,1,3,0:T(8,128)} fusion(f32[32,4,64,512]{3,2,1,0:T(8,128)S(1)} %bitcast.205, f32[32,64,4,64]{3,2,1,0:T(4,128)S(1)} %copy-done.7), kind=kOutput, calls=%fused_computation.19 | convolution fusion | flops 3221225472 | bytes 23068672 | tf_op jit(solution)/shard_map/rinj,rnjk->rik/dot_general | solution.py:64
  282.6 10.2 %fusion.89 = f32[5,512,512]{1,2,0:T(8,128)} fusion(f32[5,512,512]{1,2,0:T(8,128)} %fusion.83, f32[32,64,512]{2,1,0:T(8,128)} %param.9, f32[32,64,512,1]{2,1,3,0:T(8,128)} %fusion.10), kind=kOutput, calls=%fused_computation.65 | convolution fusion | flops 6442450944 | bytes 9437184 | tf_op jit(solution)/shard_map/dot_general | solution.py:66
  292.9 7.9 %add.108 = f32[5,512,512]{1,2,0:T(8,128)} add(f32[5,512,512]{1,2,0:T(8,128)} %copy-done.10, f32[5,512,512]{1,2,0:T(8,128)} %fusion.89) | non-fusion elementwise | flops 1310720 | bytes 15728640 | tf_op jit(solution)/shard_map/add | solution.py:89
  300.8 146.3 %all-reduce.2.cloned.1.call-done = f32[5,512,512]{1,2,0:T(8,128)} async-done(((f32[5,512,512]{1,2,0:T(8,128)}), f32[5,512,512]{1,2,0:T(8,128)}) %all-reduce.2.cloned.1.call-update) | async-done | bytes 5242896 | tf_op jit(solution)/shard_map/psum | solution.py:90
  447.1 5.9 %copy.27 = f32[5,512,512]{2,1,0:T(8,128)} copy(f32[5,512,512]{1,2,0:T(8,128)} %all-reduce.2.cloned.1.call-done) | data formatting | bytes 10485760 | tf_op jit(solution)/shard_map/psum | solution.py:90
  (84 shorter events, 7.1 us)
Async XLA Ops:
  6.5 22.9 %copy-start = (f32[16,32,512]{2,1,0:T(8,128)S(1)}, f32[16,32,512]{2,1,0:T(8,128)}, u32[]{:S(2)}) copy-start(f32[16,32,512]{2,1,0:T(8,128)} %param.7) | copy-start | bytes 3145732
  6.5 440.6 %all-reduce.2.cloned.1.call-start = ((), (), s32[]{:S(2)}) async-start(), calls=%async_computation | async-start | bytes 10485760 | tf_op jit(solution)/shard_map/psum | solution.py:90
  11.0 92.4 %collective-permute-start.2 = (f32[4,64,512]{2,1,0:T(8,128)}, f32[4,64,512]{2,1,0:T(8,128)}, u32[]{:S(2)}, u32[]{:S(2)}) collective-permute-start(f32[4,64,512]{2,1,0:T(8,128)} %gather_fusion), channel_id=1, source_target_pairs={{0,8},{8,16},{16,24},{24,0},{1,9},{9,17},{17,25},{25,1},{2,10},{10... | collective-permute-start | bytes 1572872 | tf_op jit(solution)/shard_map/ppermute | solution.py:18
  17.6 87.6 %collective-permute-start.3 = (f32[4,64,512]{2,1,0:T(8,128)}, f32[4,64,512]{2,1,0:T(8,128)}, u32[]{:S(2)}, u32[]{:S(2)}) collective-permute-start(f32[4,64,512]{2,1,0:T(8,128)} %gather_fusion.1), channel_id=1, source_target_pairs={{0,24},{8,0},{16,8},{24,16},{1,25},{9,1},{17,9},{25,17},{2,26},{10... | collective-permute-start | bytes 1572872 | tf_op jit(solution)/shard_map/ppermute | solution.py:18
  23.2 83.9 %collective-permute-start.4 = (f32[4,64,512]{2,1,0:T(8,128)}, f32[4,64,512]{2,1,0:T(8,128)}, u32[]{:S(2)}, u32[]{:S(2)}) collective-permute-start(f32[4,64,512]{2,1,0:T(8,128)} %gather_fusion.2), channel_id=1, source_target_pairs={{0,1},{1,2},{2,3},{3,4},{4,5},{5,6},{6,7},{7,0},{8,9},{9,10},{10,1... | collective-permute-start | bytes 1572872 | tf_op jit(solution)/shard_map/ppermute | solution.py:18
  26.8 82.2 %collective-permute-start.5 = (f32[4,64,512]{2,1,0:T(8,128)}, f32[4,64,512]{2,1,0:T(8,128)}, u32[]{:S(2)}, u32[]{:S(2)}) collective-permute-start(f32[4,64,512]{2,1,0:T(8,128)} %gather_fusion.3), channel_id=1, source_target_pairs={{0,7},{1,0},{2,1},{3,2},{4,3},{5,4},{6,5},{7,6},{8,15},{9,8},{10,9... | collective-permute-start | bytes 1572872 | tf_op jit(solution)/shard_map/ppermute | solution.py:18
  29.5 6.2 %copy-start.12 = (s32[5,32,4]{1,2,0:T(4,128)S(1)}, s32[5,32,4]{1,2,0:T(4,128)}, u32[]{:S(2)}) copy-start(s32[5,32,4]{1,2,0:T(4,128)} %param.11) | copy-start | bytes 7684
  29.5 6.6 %copy-start.13 = (s32[5,32]{1,0:T(8,128)S(1)}, s32[5,32]{1,0:T(8,128)}, u32[]{:S(2)}) copy-start(s32[5,32]{1,0:T(8,128)} %param.12) | copy-start | bytes 1924
  29.5 56.2 %collective-permute-start.1 = (f32[16,1,512]{2,1,0:T(1,128)S(1)}, f32[16,1,512]{2,1,0:T(1,128)S(1)}, u32[]{:S(2)}, u32[]{:S(2)}) collective-permute-start(f32[16,1,512]{2,1,0:T(1,128)S(1)} %slice.94), channel_id=1, source_target_pairs={{1,0},{2,1},{3,2},{4,3},{5,4},{6,5},{7,6},{9,8},{10,9},{11,10},{12... | collective-permute-start | bytes 98312 | tf_op jit(solution)/shard_map/ppermute | solution.py:12
  64.9 3.6 copy-start.11
  68.4 2.2 copy-start.4
  70.6 2.9 copy-start.5
  73.5 3.0 copy-start.1
  76.6 3.0 copy-start.2
  79.5 2.9 copy-start.3
  85.7 6.7 %collective-permute-start = (f32[1,32,512]{2,1,0:T(8,128)S(1)}, f32[1,32,512]{2,1,0:T(8,128)S(1)}, u32[]{:S(2)}, u32[]{:S(2)}) collective-permute-start(f32[1,32,512]{2,1,0:T(8,128)S(1)} %slice.91), channel_id=1, source_target_pairs={{8,0},{16,8},{24,16},{9,1},{17,9},{25,17},{10,2},{18,10},{26,18},{... | collective-permute-start | bytes 196616 | tf_op jit(solution)/shard_map/ppermute | solution.py:12
  101.0 2.4 copy-start.10
  136.4 14.0 %copy-start.9 = (f32[32,64,512]{2,1,0:T(8,128)S(1)}, f32[32,64,512]{2,1,0:T(8,128)}, u32[]{:S(2)}) copy-start(f32[32,64,512]{2,1,0:T(8,128)} %param.9) | copy-start | bytes 12582916
  196.5 26.5 %slice-start.4 = ((s8[16777216]{0:T(1024)(128)(4,1)}), s8[4194304]{0:T(1024)(128)(4,1)S(1)}, s32[]{:S(2)}) async-start(s8[16777216]{0:T(1024)(128)(4,1)} %bitcast.208), calls=%async_computation.5 | async-start | bytes 8388608
  196.5 26.5 %slice-start.5 = ((s8[16777216]{0:T(1024)(128)(4,1)}), s8[4194304]{0:T(1024)(128)(4,1)S(1)}, s32[]{:S(2)}) async-start(s8[16777216]{0:T(1024)(128)(4,1)} %bitcast.208), calls=%async_computation.6 | async-start | bytes 8388608
  196.5 26.5 %slice-start.6 = ((s8[16777216]{0:T(1024)(128)(4,1)}), s8[4194304]{0:T(1024)(128)(4,1)S(1)}, s32[]{:S(2)}) async-start(s8[16777216]{0:T(1024)(128)(4,1)} %bitcast.208), calls=%async_computation.7 | async-start | bytes 8388608
  212.6 10.4 %slice-start.7 = ((s8[16777216]{0:T(1024)(128)(4,1)}), s8[4194304]{0:T(1024)(128)(4,1)S(1)}, s32[]{:S(2)}) async-start(s8[16777216]{0:T(1024)(128)(4,1)} %bitcast.208), calls=%async_computation.8 | async-start | bytes 8388608
  212.6 10.4 %copy-start.6 = (f32[32,64,4,64]{3,2,1,0:T(4,128)S(1)}, f32[32,64,4,64]{3,2,1,0:T(4,128)}, u32[]{:S(2)}) copy-start(f32[32,64,4,64]{3,2,1,0:T(4,128)} %broadcast_multiply_fusion.2) | copy-start | bytes 6291460
  235.1 10.4 %copy-start.8 = (f32[32,64,4,64]{3,2,1,0:T(4,128)S(1)}, f32[32,64,4,64]{3,2,1,0:T(4,128)}, u32[]{:S(2)}) copy-start(f32[32,64,4,64]{3,2,1,0:T(4,128)} %broadcast_multiply_fusion.1) | copy-start | bytes 6291460
  245.5 25.3 %slice-start = ((s8[16777216]{0:T(1024)(128)(4,1)}), s8[4194304]{0:T(1024)(128)(4,1)S(1)}, s32[]{:S(2)}) async-start(s8[16777216]{0:T(1024)(128)(4,1)} %bitcast.203), calls=%async_computation.1 | async-start | bytes 8388608
  245.5 25.3 %slice-start.1 = ((s8[16777216]{0:T(1024)(128)(4,1)}), s8[4194304]{0:T(1024)(128)(4,1)S(1)}, s32[]{:S(2)}) async-start(s8[16777216]{0:T(1024)(128)(4,1)} %bitcast.203), calls=%async_computation.2 | async-start | bytes 8388608
  245.5 25.3 %slice-start.2 = ((s8[16777216]{0:T(1024)(128)(4,1)}), s8[4194304]{0:T(1024)(128)(4,1)S(1)}, s32[]{:S(2)}) async-start(s8[16777216]{0:T(1024)(128)(4,1)} %bitcast.203), calls=%async_computation.3 | async-start | bytes 8388608
  260.2 10.6 %slice-start.3 = ((s8[16777216]{0:T(1024)(128)(4,1)}), s8[4194304]{0:T(1024)(128)(4,1)S(1)}, s32[]{:S(2)}) async-start(s8[16777216]{0:T(1024)(128)(4,1)} %bitcast.203), calls=%async_computation.4 | async-start | bytes 8388608
  260.2 10.6 %copy-start.7 = (f32[32,64,4,64]{3,2,1,0:T(4,128)S(1)}, f32[32,64,4,64]{3,2,1,0:T(4,128)}, u32[]{:S(2)}) copy-start(f32[32,64,4,64]{3,2,1,0:T(4,128)} %broadcast_multiply_fusion) | copy-start | bytes 6291460
Sparse Core Ops, SparseCore 0:
  301.0 146.1 all-reduce.1
where the time goes:
time: 468 us; the launch traced here: 460 us
  waiting for transfers between devices  149 us (32%)
  local copies, waits for them, and re-layouts  132 us (28%)
  matrix products  131 us (28%)
  other arithmetic  23.7 us (5%)
  between operations  14.2 us (3%)
  starting transfers between devices  10.5 us (2%)
    psum x1, waiting for transfers between devices, body(): return lax.psum(partial_terms, ('gx', 'gy'))  146 us
    dot_general x5, matrix products, package_terms(): image = jnp.einsum('rinj,rnjk->rik', matrices, picked, precision=highest)  68.6 us
    gather x5, local copies, waits for them, and re-layouts, package_terms(): picked = table[columns[term_idx]]  63.7 us
    dot_general x5, matrix products, package_terms(): lax.dot_general(owned.reshape(-1, width), image.reshape(-1, width), (((0,...  49.6 us
    another operation x5, local copies, waits for them, and re-layouts, package_terms(): blocks[term_idx].reshape(row_count, block, entries, block)  23.8 us
    mul x5, other arithmetic, package_terms(): blocks[term_idx].reshape(row_count, block, entries, block)  14.7 us
    unnamed x48, local copies, waits for them, and re-layouts  13 us
    dot_general x6, matrix products, weighted_gram(): lax.dot_general(flat, scaled, (((0,), (0,)), ((), ())), precision=highest...  12.7 us
  transfers between devices with their start and end apart: 7, of which 2 were waited for; matrix products, arithmetic and copies ran while one was open for 18% of the time, Pallas kernels for 0%

commit v1 on v0

--- a/solution.py
+++ b/solution.py
@@ -87,7 +87,7 @@
     )
     partial_terms = die_terms(die_basis, die_coeff, next_x_row, next_y_col)
     partial_terms = partial_terms + package_terms(pkg_basis, table, columns, counts, pkg_blocks)
-    return lax.psum(partial_terms, ("gx", "gy"))
+    return lax.psum(lax.psum(partial_terms, axis_name="gy"), axis_name="gx")
 
 
 def solution(mesh):

time: 468 us -> 607 us (1.30)
  waiting for transfers between devices: 149 us -> 285 us
    psum x1 -> x2, waiting for transfers between devices: 146 us -> 282 us  [body(): return lax.psum(lax.psum(partial_terms, axis_name='gy'), axis_name='gx')]
    unnamed x48 -> x44, local copies, waits for them, and re-layouts: 13 us -> 13 us
  transfers between devices with their start and end apart: 7 -> 8, of which waited for: 2 -> 3; matrix products, arithmetic and copies ran while one was open for 18% -> 14% of each run, Pallas kernels for 0% -> 0%
where the time goes in v1:
time: 607 us; the launch traced here: 599 us
  waiting for transfers between devices  285 us (47%)
  matrix products  134 us (22%)
  local copies, waits for them, and re-layouts  132 us (22%)
  other arithmetic  23.8 us (4%)
  between operations  14.2 us (2%)
  starting transfers between devices  10.5 us (2%)
    psum x2, waiting for transfers between devices, body(): return lax.psum(lax.psum(partial_terms, axis_name='gy'), axis_name='gx')  282 us
    dot_general x5, matrix products, package_terms(): image = jnp.einsum('rinj,rnjk->rik', matrices, picked, precision=highest)  71.7 us
    gather x5, local copies, waits for them, and re-layouts, package_terms(): picked = table[columns[term_idx]]  63.7 us
    dot_general x5, matrix products, package_terms(): lax.dot_general(owned.reshape(-1, width), image.reshape(-1, width), (((0,...  49.6 us
    another operation x5, local copies, waits for them, and re-layouts, package_terms(): blocks[term_idx].reshape(row_count, block, entries, block)  23.8 us
    mul x5, other arithmetic, package_terms(): blocks[term_idx].reshape(row_count, block, entries, block)  14.7 us
    unnamed x44, local copies, waits for them, and re-layouts  13 us
    dot_general x6, matrix products, weighted_gram(): lax.dot_general(flat, scaled, (((0,), (0,)), ((), ())), precision=highest...  12.8 us
  transfers between devices with their start and end apart: 8, of which 3 were waited for; matrix products, arithmetic and copies ran while one was open for 14% of the time, Pallas kernels for 0%

profile of v1, /device:TPU:0, one launch (start us, length us, event | category | flops | bytes accessed | tf_op | source)
XLA Modules:
  0.0 599.2 jit_solution(4853784650961317529)
XLA Ops:
  7.4 3.6 gather_fusion
  11.0 3.1 collective-permute-start.2
  14.0 3.6 gather_fusion.1
  17.6 2.0 collective-permute-start.3
  19.6 3.6 gather_fusion.2
  23.2 3.6 gather_fusion.3
  26.8 2.6 collective-permute-start.5
  30.8 4.9 constant_dynamic-update-slice_fusion.4
  36.1 8.0 %fusion.120 = (f32[1,32,64,256]{3,2,1,0:T(8,128)S(1)}, f32[1,32,64,256]{3,2,1,0:T(8,128)}, f32[1,32,64,256]{3,2,1,0:T(8,128)}, f32[1,32,64,256]{3,2,1,0:T(8,128)}, f32[1,32,64,256]{3,2,1,0:T(8,128)}) fusion(f32[5,32,64,256]{3,2,1,0:T(8,128)} %param.13), kind=kLoop, calls=%fused_computation.128 | loop fusion | bytes 20971520 | tf_op jit(solution)/shard_map/slice | solution.py:62
  44.0 5.1 reshape_squeeze.22
  49.3 5.1 reshape_squeeze.10
  54.3 5.1 reshape_squeeze.23
  59.8 5.1 reshape_squeeze.24
  64.9 3.5 reshape_squeeze.25
  68.5 2.0 fusion.35
  70.6 2.9 broadcast_multiply_fusion.3
  73.6 3.0 broadcast_multiply_fusion.4
  76.6 2.9 broadcast_multiply_fusion.2
  79.6 2.9 broadcast_multiply_fusion.1
  82.5 3.0 broadcast_multiply_fusion
  87.2 2.2 fusion.59
  89.5 3.0 collective-permute-done
  92.5 2.2 fusion.41
  94.6 2.2 fusion.47
  96.9 2.0 fusion.53
  98.8 2.2 fusion.98
  101.0 2.3 copy-done.8
  105.3 1.9 constant_dynamic-update-slice_fusion.2
  107.2 1.9 constant_dynamic-update-slice_fusion.1
  110.9 12.9 %gather_fusion.5 = f32[128,64,512]{2,1,0:T(8,128)} fusion(f32[48,64,512]{2,1,0:T(8,128)} %constant_dynamic-update-slice_fusion, s32[1024]{0:T(1024)S(1)} %get-tuple-element.32), kind=kCustom, calls=%fused_computation.5 | custom fusion | bytes 33554944 | tf_op jit(solution)/shard_map/gather | solution.py:57
  123.8 12.7 %gather_fusion.4 = f32[128,64,512]{2,1,0:T(8,128)} fusion(f32[48,64,512]{2,1,0:T(8,128)} %constant_dynamic-update-slice_fusion, s32[1024]{0:T(1024)S(1)} %pad_clamp_fusion.4), kind=kCustom, calls=%fused_computation.4 | custom fusion | bytes 33554944 | tf_op jit(solution)/shard_map/gather | solution.py:57
  136.5 13.9 %fusion.18 = f32[32,64,512,1]{2,1,3,0:T(8,128)S(1)} fusion(f32[32,4,64,512]{3,2,1,0:T(8,128)} %bitcast.211, f32[32,64,4,64]{3,2,1,0:T(4,128)} %broadcast_multiply_fusion.4), kind=kOutput, calls=%fused_computation.27 | convolution fusion | flops 3221225472 | bytes 23068672 | tf_op jit(solution)/shard_map/rinj,rnjk->rik/dot_general | solution.py:64
  150.4 8.0 %fusion.65 = f32[5,512,512]{1,2,0:T(8,128)} fusion(f32[32,64,512]{2,1,0:T(8,128)S(1)} %copy-done.7, f32[32,64,512,1]{2,1,3,0:T(8,128)S(1)} %fusion.18), kind=kOutput, calls=%fused_computation.57 | convolution fusion | flops 6442450944 | bytes 9437184 | tf_op jit(solution)/shard_map/dot_general | solution.py:66
  158.4 12.7 %gather_fusion.6 = f32[128,64,512]{2,1,0:T(8,128)} fusion(f32[48,64,512]{2,1,0:T(8,128)} %constant_dynamic-update-slice_fusion, s32[1024]{0:T(1024)S(1)} %get-tuple-element.31), kind=kCustom, calls=%fused_computation.6 | custom fusion | bytes 33554944 | tf_op jit(solution)/shard_map/gather | solution.py:57
  171.1 12.7 %gather_fusion.7 = f32[128,64,512]{2,1,0:T(8,128)} fusion(f32[48,64,512]{2,1,0:T(8,128)} %constant_dynamic-update-slice_fusion, s32[1024]{0:T(1024)S(1)} %get-tuple-element.30), kind=kCustom, calls=%fused_computation.7 | custom fusion | bytes 33554944 | tf_op jit(solution)/shard_map/gather | solution.py:57
  183.8 12.9 %gather_fusion.8 = f32[128,64,512]{2,1,0:T(8,128)} fusion(f32[48,64,512]{2,1,0:T(8,128)} %constant_dynamic-update-slice_fusion, s32[1024]{0:T(1024)S(1)} %get-tuple-element.29), kind=kCustom, calls=%fused_computation.8 | custom fusion | bytes 33554944 | tf_op jit(solution)/shard_map/gather | solution.py:57
  196.6 16.0 %fusion.16 = f32[32,64,512,1]{2,1,3,0:T(8,128)} fusion(f32[32,4,64,512]{3,2,1,0:T(8,128)} %bitcast.206, f32[32,64,4,64]{3,2,1,0:T(4,128)} %broadcast_multiply_fusion.3), kind=kOutput, calls=%fused_computation.25 | convolution fusion | flops 3221225472 | bytes 23068672 | tf_op jit(solution)/shard_map/rinj,rnjk->rik/dot_general | solution.py:64
  212.7 10.4 %fusion.71 = f32[5,512,512]{1,2,0:T(8,128)} fusion(f32[5,512,512]{1,2,0:T(8,128)} %fusion.65, f32[32,64,512]{2,1,0:T(8,128)} %param.9, f32[32,64,512,1]{2,1,3,0:T(8,128)} %fusion.16), kind=kOutput, calls=%fused_computation.59 | convolution fusion | flops 6442450944 | bytes 9437184 | tf_op jit(solution)/shard_map/dot_general | solution.py:66
  223.1 13.6 %fusion.14 = f32[32,64,512,1]{2,1,3,0:T(8,128)} fusion(f32[32,4,64,512]{3,2,1,0:T(8,128)S(1)} %bitcast.210, f32[32,64,4,64]{3,2,1,0:T(4,128)} %broadcast_multiply_fusion.2), kind=kOutput, calls=%fused_computation.23 | convolution fusion | flops 3221225472 | bytes 23068672 | tf_op jit(solution)/shard_map/rinj,rnjk->rik/dot_general | solution.py:64
  236.7 10.4 %fusion.77 = f32[5,512,512]{1,2,0:T(8,128)} fusion(f32[5,512,512]{1,2,0:T(8,128)} %fusion.71, f32[32,64,512]{2,1,0:T(8,128)} %param.9, f32[32,64,512,1]{2,1,3,0:T(8,128)} %fusion.14), kind=kOutput, calls=%fused_computation.61 | convolution fusion | flops 6442450944 | bytes 9437184 | tf_op jit(solution)/shard_map/dot_general | solution.py:66
  247.1 14.7 %fusion.12 = f32[32,64,512,1]{2,1,3,0:T(8,128)} fusion(f32[32,4,64,512]{3,2,1,0:T(8,128)} %bitcast.207, f32[32,64,4,64]{3,2,1,0:T(4,128)S(1)} %copy-done.6), kind=kOutput, calls=%fused_computation.21 | convolution fusion | flops 3221225472 | bytes 23068672 | tf_op jit(solution)/shard_map/rinj,rnjk->rik/dot_general | solution.py:64
  261.8 10.6 %fusion.83 = f32[5,512,512]{1,2,0:T(8,128)} fusion(f32[5,512,512]{1,2,0:T(8,128)} %fusion.77, f32[32,64,512]{2,1,0:T(8,128)} %param.9, f32[32,64,512,1]{2,1,3,0:T(8,128)} %fusion.12), kind=kOutput, calls=%fused_computation.63 | convolution fusion | flops 6442450944 | bytes 9437184 | tf_op jit(solution)/shard_map/dot_general | solution.py:66
  272.4 13.4 %fusion.10 = f32[32,64,512,1]{2,1,3,0:T(8,128)} fusion(f32[32,4,64,512]{3,2,1,0:T(8,128)S(1)} %bitcast.205, f32[32,64,4,64]{3,2,1,0:T(4,128)} %broadcast_multiply_fusion), kind=kOutput, calls=%fused_computation.19 | convolution fusion | flops 3221225472 | bytes 23068672 | tf_op jit(solution)/shard_map/rinj,rnjk->rik/dot_general | solution.py:64
  285.8 10.2 %fusion.89 = f32[5,512,512]{1,2,0:T(8,128)} fusion(f32[5,512,512]{1,2,0:T(8,128)} %fusion.83, f32[32,64,512]{2,1,0:T(8,128)} %param.9, f32[32,64,512,1]{2,1,3,0:T(8,128)} %fusion.10), kind=kOutput, calls=%fused_computation.65 | convolution fusion | flops 6442450944 | bytes 9437184 | tf_op jit(solution)/shard_map/dot_general | solution.py:66
  296.1 7.9 %add.110 = f32[5,512,512]{1,2,0:T(8,128)} add(f32[5,512,512]{1,2,0:T(8,128)} %copy-done.8, f32[5,512,512]{1,2,0:T(8,128)} %fusion.89) | non-fusion elementwise | flops 1310720 | bytes 15728640 | tf_op jit(solution)/shard_map/add | solution.py:89
  304.1 90.6 %all-reduce.3.cloned.1.call-done = f32[5,512,512]{1,2,0:T(8,128)} async-done(((f32[5,512,512]{1,2,0:T(8,128)}), f32[5,512,512]{1,2,0:T(8,128)}) %all-reduce.3.cloned.1.call-update) | async-done | bytes 5242896 | tf_op jit(solution)/shard_map/psum | solution.py:90
  394.7 191.4 %all-reduce.5.cloned.1.call-done = f32[5,512,512]{1,2,0:T(8,128)} async-done(((f32[5,512,512]{1,2,0:T(8,128)}), f32[5,512,512]{1,2,0:T(8,128)}) %all-reduce.5.cloned.1.call-update) | async-done | bytes 5242896 | tf_op jit(solution)/shard_map/psum | solution.py:90
  586.1 5.9 copy.27
  (83 shorter events, 9.0 us)
Async XLA Ops:
  6.5 22.9 %copy-start = (f32[16,32,512]{2,1,0:T(8,128)S(1)}, f32[16,32,512]{2,1,0:T(8,128)}, u32[]{:S(2)}) copy-start(f32[16,32,512]{2,1,0:T(8,128)} %param.7) | copy-start | bytes 3145732
  6.5 388.1 %all-reduce.3.cloned.1.call-start = ((), (), s32[]{:S(2)}) async-start(), calls=%async_computation | async-start | bytes 10485760 | tf_op jit(solution)/shard_map/psum | solution.py:90
  11.0 92.4 %collective-permute-start.2 = (f32[4,64,512]{2,1,0:T(8,128)}, f32[4,64,512]{2,1,0:T(8,128)}, u32[]{:S(2)}, u32[]{:S(2)}) collective-permute-start(f32[4,64,512]{2,1,0:T(8,128)} %gather_fusion), channel_id=1, source_target_pairs={{0,8},{8,16},{16,24},{24,0},{1,9},{9,17},{17,25},{25,1},{2,10},{10... | collective-permute-start | bytes 1572872 | tf_op jit(solution)/shard_map/ppermute | solution.py:18
  17.6 87.7 %collective-permute-start.3 = (f32[4,64,512]{2,1,0:T(8,128)}, f32[4,64,512]{2,1,0:T(8,128)}, u32[]{:S(2)}, u32[]{:S(2)}) collective-permute-start(f32[4,64,512]{2,1,0:T(8,128)} %gather_fusion.1), channel_id=1, source_target_pairs={{0,24},{8,0},{16,8},{24,16},{1,25},{9,1},{17,9},{25,17},{2,26},{10... | collective-permute-start | bytes 1572872 | tf_op jit(solution)/shard_map/ppermute | solution.py:18
  23.2 83.9 %collective-permute-start.4 = (f32[4,64,512]{2,1,0:T(8,128)}, f32[4,64,512]{2,1,0:T(8,128)}, u32[]{:S(2)}, u32[]{:S(2)}) collective-permute-start(f32[4,64,512]{2,1,0:T(8,128)} %gather_fusion.2), channel_id=1, source_target_pairs={{0,1},{1,2},{2,3},{3,4},{4,5},{5,6},{6,7},{7,0},{8,9},{9,10},{10,1... | collective-permute-start | bytes 1572872 | tf_op jit(solution)/shard_map/ppermute | solution.py:18
  26.8 82.2 %collective-permute-start.5 = (f32[4,64,512]{2,1,0:T(8,128)}, f32[4,64,512]{2,1,0:T(8,128)}, u32[]{:S(2)}, u32[]{:S(2)}) collective-permute-start(f32[4,64,512]{2,1,0:T(8,128)} %gather_fusion.3), channel_id=1, source_target_pairs={{0,7},{1,0},{2,1},{3,2},{4,3},{5,4},{6,5},{7,6},{8,15},{9,8},{10,9... | collective-permute-start | bytes 1572872 | tf_op jit(solution)/shard_map/ppermute | solution.py:18
  29.4 6.2 %copy-start.10 = (s32[5,32,4]{1,2,0:T(4,128)S(1)}, s32[5,32,4]{1,2,0:T(4,128)}, u32[]{:S(2)}) copy-start(s32[5,32,4]{1,2,0:T(4,128)} %param.11) | copy-start | bytes 7684
  29.5 6.6 %copy-start.11 = (s32[5,32]{1,0:T(8,128)S(1)}, s32[5,32]{1,0:T(8,128)}, u32[]{:S(2)}) copy-start(s32[5,32]{1,0:T(8,128)} %param.12) | copy-start | bytes 1924
  29.5 56.3 %collective-permute-start.1 = (f32[16,1,512]{2,1,0:T(1,128)S(1)}, f32[16,1,512]{2,1,0:T(1,128)S(1)}, u32[]{:S(2)}, u32[]{:S(2)}) collective-permute-start(f32[16,1,512]{2,1,0:T(1,128)S(1)} %slice.94), channel_id=1, source_target_pairs={{1,0},{2,1},{3,2},{4,3},{5,4},{6,5},{7,6},{9,8},{10,9},{11,10},{12... | collective-permute-start | bytes 98312 | tf_op jit(solution)/shard_map/ppermute | solution.py:12
  64.9 3.6 copy-start.9
  68.4 2.2 copy-start.4
  70.6 2.9 copy-start.5
  73.6 3.0 copy-start.1
  76.6 3.0 copy-start.2
  79.6 2.9 copy-start.3
  85.8 6.7 %collective-permute-start = (f32[1,32,512]{2,1,0:T(8,128)S(1)}, f32[1,32,512]{2,1,0:T(8,128)S(1)}, u32[]{:S(2)}, u32[]{:S(2)}) collective-permute-start(f32[1,32,512]{2,1,0:T(8,128)S(1)} %slice.91), channel_id=1, source_target_pairs={{8,0},{16,8},{24,16},{9,1},{17,9},{25,17},{10,2},{18,10},{26,18},{... | collective-permute-start | bytes 196616 | tf_op jit(solution)/shard_map/ppermute | solution.py:12
  101.0 2.4 copy-start.8
  136.4 14.0 %copy-start.7 = (f32[32,64,512]{2,1,0:T(8,128)S(1)}, f32[32,64,512]{2,1,0:T(8,128)}, u32[]{:S(2)}) copy-start(f32[32,64,512]{2,1,0:T(8,128)} %param.9) | copy-start | bytes 12582916
  196.6 26.5 %slice-start.4 = ((s8[16777216]{0:T(1024)(128)(4,1)}), s8[4194304]{0:T(1024)(128)(4,1)S(1)}, s32[]{:S(2)}) async-start(s8[16777216]{0:T(1024)(128)(4,1)} %bitcast.208), calls=%async_computation.6 | async-start | bytes 8388608
  196.6 26.5 %slice-start.5 = ((s8[16777216]{0:T(1024)(128)(4,1)}), s8[4194304]{0:T(1024)(128)(4,1)S(1)}, s32[]{:S(2)}) async-start(s8[16777216]{0:T(1024)(128)(4,1)} %bitcast.208), calls=%async_computation.7 | async-start | bytes 8388608
  196.6 26.5 %slice-start.6 = ((s8[16777216]{0:T(1024)(128)(4,1)}), s8[4194304]{0:T(1024)(128)(4,1)S(1)}, s32[]{:S(2)}) async-start(s8[16777216]{0:T(1024)(128)(4,1)} %bitcast.208), calls=%async_computation.8 | async-start | bytes 8388608
  212.7 10.4 %slice-start.7 = ((s8[16777216]{0:T(1024)(128)(4,1)}), s8[4194304]{0:T(1024)(128)(4,1)S(1)}, s32[]{:S(2)}) async-start(s8[16777216]{0:T(1024)(128)(4,1)} %bitcast.208), calls=%async_computation.9 | async-start | bytes 8388608
  236.7 10.4 %copy-start.6 = (f32[32,64,4,64]{3,2,1,0:T(4,128)S(1)}, f32[32,64,4,64]{3,2,1,0:T(4,128)}, u32[]{:S(2)}) copy-start(f32[32,64,4,64]{3,2,1,0:T(4,128)} %broadcast_multiply_fusion.1) | copy-start | bytes 6291460
  247.1 25.3 %slice-start = ((s8[16777216]{0:T(1024)(128)(4,1)}), s8[4194304]{0:T(1024)(128)(4,1)S(1)}, s32[]{:S(2)}) async-start(s8[16777216]{0:T(1024)(128)(4,1)} %bitcast.203), calls=%async_computation.2 | async-start | bytes 8388608
  247.1 25.3 %slice-start.1 = ((s8[16777216]{0:T(1024)(128)(4,1)}), s8[4194304]{0:T(1024)(128)(4,1)S(1)}, s32[]{:S(2)}) async-start(s8[16777216]{0:T(1024)(128)(4,1)} %bitcast.203), calls=%async_computation.3 | async-start | bytes 8388608
  247.1 25.3 %slice-start.2 = ((s8[16777216]{0:T(1024)(128)(4,1)}), s8[4194304]{0:T(1024)(128)(4,1)S(1)}, s32[]{:S(2)}) async-start(s8[16777216]{0:T(1024)(128)(4,1)} %bitcast.203), calls=%async_computation.4 | async-start | bytes 8388608
  261.8 10.6 %slice-start.3 = ((s8[16777216]{0:T(1024)(128)(4,1)}), s8[4194304]{0:T(1024)(128)(4,1)S(1)}, s32[]{:S(2)}) async-start(s8[16777216]{0:T(1024)(128)(4,1)} %bitcast.203), calls=%async_computation.5 | async-start | bytes 8388608
  304.0 282.0 %all-reduce.5.cloned.1.call-start = ((), (), s32[]{:S(2)}) async-start(), calls=%async_computation.1 | async-start | bytes 10485760 | tf_op jit(solution)/shard_map/psum | solution.py:90
Sparse Core Ops, SparseCore 0:
  304.2 90.4 all-reduce.2
  397.0 188.9 all-reduce.4
